TPU v7x, 32 devices: a whole 2x2x4 slice. The times are simulated.
32 devices in a mesh: section: 2 (over core), dp: 4 (over z), tensor: 4 (over y, x).
Axes of the slice: x: 2, y: 2, z: 4, core: 2. Of those that a mesh axis runs over, the one named last changes fastest.
Arguments:
- boundary: bfloat16 [2, 4, 196, 24, 512], P('section', None, 'tensor', 'dp'), may hold values from -11 to 11
- live: int32 [4, 4], P(None, 'dp'), may hold values from 1 to 6, 18 in all within a row
- w_qkv: bfloat16 [2, 512, 3, 512], P('section', 'dp', None, 'tensor'), may hold values from -0.25 to 0.25
- w_proj: bfloat16 [2, 512, 512], P('section', 'tensor', 'dp'), may hold values from -1 to 1
- w_fc1: bfloat16 [2, 512, 2048], P('section', 'dp', 'tensor'), may hold values from -0.25 to 0.25
- w_fc2: bfloat16 [2, 2048, 512], P('section', 'tensor', 'dp'), may hold values from -0.125 to 0.125
- gains: bfloat16 [2, 2, 512], P('section', None, 'dp'), may hold values from 0.25 to 1.75
- biases: bfloat16 [2, 10, 512], P('section', None, 'dp'), may hold values from -3 to 3
Outputs:
- results: float32 [2, 4, 196, 24, 512], P('section', None, 'tensor', 'dp')
- grad_qkv: float32 [2, 512, 3, 512], P('section', 'dp', None, 'tensor')
- grad_proj: float32 [2, 512, 512], P('section', 'tensor', 'dp')
- grad_fc1: float32 [2, 512, 2048], P('section', 'dp', 'tensor')
- grad_fc2: float32 [2, 2048, 512], P('section', 'tensor', 'dp')
- grad_gains: float32 [2, 2, 512], P('section', None, ('dp', 'tensor'))
- grad_biases: float32 [2, 10, 512], P('section', None, ('dp', 'tensor'))
Inputs may be any that keep to these rules, and one draw needn't show every extreme that they name: live[m, j] of the 6 slots of data-axis index j are used in micro-batch m, the first ones; each micro-batch uses 3 * 6 * 1 images, and in each some index uses all 6.
All inputs are finite; a program needn't handle non-finite values. No bound on the sum of `live` on one device may be relied on, other than what follows from the above.
Results may differ from a plain program's by a relative error of at most 0.033.
Values may be sent and summed in bfloat16 or wider, within the bound.
No kernel may reach another device: no remote copies, remote signals or barrier semaphores. Data moves between devices by JAX's collectives and lax.ppermute only.
A program may use at most 256 MiB of HBM per device.

v0:
```python
import jax
import jax.numpy as jnp
from jax import lax
from jax.sharding import PartitionSpec as P

HEAD_DIM = 32
FF = 2048
GRID = 14
WIN = 7
SHIFT = 3


EPSILON = 1e-05


def from_behind(x, axis, by):
    devices = lax.axis_size(axis)
    pairs = [(i, i + by) for i in range(devices) if 0 <= i + by < devices]
    return lax.ppermute(x, axis, pairs)


def layer_norm(values, gain, offset):
    centre = jnp.mean(values, axis=-1, keepdims=True)
    centred = values - centre
    inverse = lax.rsqrt(jnp.mean(centred * centred, axis=-1, keepdims=True) + EPSILON)
    normal = centred * inverse
    return (normal * gain + offset, normal, inverse)


def norm_back(grad, normal, inverse, gain):
    scaled = grad * gain
    return inverse * (
        scaled
        - jnp.mean(scaled, axis=-1, keepdims=True)
        - normal * jnp.mean(scaled * normal, axis=-1, keepdims=True)
    )


def exact_gelu(values):
    return jax.nn.gelu(values, approximate=False)


def region_keep(shifted, images):
    per_side = GRID // WIN
    coord = jnp.arange(GRID)
    band = (coord >= GRID - WIN).astype(jnp.int32) + (coord >= GRID - SHIFT).astype(jnp.int32)
    region = (band[:, None] * 3 + band[None, :]).reshape(per_side, WIN, per_side, WIN)
    region = region.transpose(0, 2, 1, 3).reshape(per_side * per_side, WIN * WIN)
    allowed = (region[:, :, None] == region[:, None, :]).astype(jnp.float32)
    allowed = jnp.where(shifted, allowed, jnp.ones_like(allowed))
    allowed = jnp.broadcast_to(allowed[None], (images, per_side * per_side, WIN * WIN, WIN * WIN))
    return allowed.reshape(images * per_side * per_side, 1, WIN * WIN, WIN * WIN)


def to_windows(values, shifted):
    images, channels = (values.shape[1], values.shape[2])
    token_grid = values.reshape(GRID, GRID, images, channels)
    token_grid = jnp.where(shifted, jnp.roll(token_grid, (-SHIFT, -SHIFT), (0, 1)), token_grid)
    per_side = GRID // WIN
    token_grid = token_grid.reshape(per_side, WIN, per_side, WIN, images, channels)
    return token_grid.transpose(4, 0, 2, 1, 3, 5).reshape(
        images * per_side * per_side, WIN * WIN, channels
    )


def from_windows(values, images, shifted):
    per_side = GRID // WIN
    channels = values.shape[-1]
    token_grid = values.reshape(images, per_side, per_side, WIN, WIN, channels)
    token_grid = token_grid.transpose(1, 3, 2, 4, 0, 5).reshape(GRID, GRID, images, channels)
    token_grid = jnp.where(shifted, jnp.roll(token_grid, (SHIFT, SHIFT), (0, 1)), token_grid)
    return token_grid.reshape(GRID * GRID, images, channels)


def attend(windows, allowed):
    score_scale = HEAD_DIM ** (-0.5)
    scores = (
        jnp.einsum(
            "wqhe,wkhe->whqk",
            windows[:, :, 0],
            windows[:, :, 1],
            preferred_element_type=jnp.float32,
        )
        * score_scale
    )
    weights = jnp.exp(scores) * allowed
    row_total = jnp.sum(weights, axis=-1, keepdims=True)
    softmax_low = (weights / row_total).astype(jnp.bfloat16)
    output = jnp.einsum(
        "whqk,wkhe->wqhe", softmax_low, windows[:, :, 2], preferred_element_type=jnp.float32
    )
    return (output.astype(jnp.bfloat16), jnp.log(row_total))


def attend_back(windows, log_total, grad_windows, allowed):
    score_scale = HEAD_DIM ** (-0.5)
    query_rows = windows[:, :, 0]
    key_rows = windows[:, :, 1]
    scores = (
        jnp.einsum("wqhe,wkhe->whqk", query_rows, key_rows, preferred_element_type=jnp.float32)
        * score_scale
    )
    softmax_full = jnp.exp(scores - log_total) * allowed
    softmax_low = softmax_full.astype(jnp.bfloat16)
    grad_value = jnp.einsum(
        "whqk,wqhe->wkhe", softmax_low, grad_windows, preferred_element_type=jnp.float32
    )
    grad_probs = jnp.einsum(
        "wqhe,wkhe->whqk", grad_windows, windows[:, :, 2], preferred_element_type=jnp.float32
    )
    centre = jnp.sum(softmax_full * grad_probs, axis=-1, keepdims=True)
    grad_scores = (softmax_full * (grad_probs - centre) * score_scale).astype(jnp.bfloat16)
    grad_query = jnp.einsum(
        "whqk,wkhe->wqhe", grad_scores, key_rows, preferred_element_type=jnp.float32
    )
    grad_key = jnp.einsum(
        "whqk,wqhe->wkhe", grad_scores, query_rows, preferred_element_type=jnp.float32
    )
    return (grad_query, grad_key, grad_value)


def split_vectors(gain_rows, bias_rows, tensor_index, head_cols, hidden_cols):
    gain_full = gain_rows.astype(jnp.float32)
    bias_full = bias_rows.astype(jnp.float32)
    query_bias = lax.dynamic_slice_in_dim(bias_full[1], tensor_index * head_cols, head_cols)
    value_bias = lax.dynamic_slice_in_dim(bias_full[2], tensor_index * head_cols, head_cols)
    qkv_bias = jnp.stack([query_bias, jnp.zeros_like(query_bias), value_bias])
    fc_bias = lax.dynamic_slice_in_dim(
        bias_full[6:].reshape(-1), tensor_index * hidden_cols, hidden_cols
    )
    return (
        gain_full[0],
        bias_full[0],
        qkv_bias,
        bias_full[3],
        gain_full[1],
        bias_full[4],
        fc_bias,
        bias_full[5],
    )


def layer_forward(inputs, matrices, vectors, shifted, allowed):
    w_qkv, w_proj, w_fc1, w_fc2 = matrices
    gain_a, offset_a, qkv_bias, out_bias, gain_b, offset_b, fc_bias, last_bias = vectors
    local_tokens, slots, width = inputs.shape
    head_cols = w_qkv.shape[2]
    residual = inputs.astype(jnp.float32)
    normed, normal_a, inverse_a = layer_norm(residual, gain_a, offset_a)
    attn_input = lax.all_gather(normed.astype(jnp.bfloat16), "tensor", axis=0, tiled=True)
    tokens = attn_input.shape[0]
    projected = (
        jnp.einsum("tsd,dch->tsch", attn_input, w_qkv, preferred_element_type=jnp.float32)
        + qkv_bias
    )
    windows = to_windows(
        projected.astype(jnp.bfloat16).reshape(tokens, slots, 3 * head_cols), shifted
    )
    windows = windows.reshape(-1, WIN * WIN, 3, head_cols // HEAD_DIM, HEAD_DIM)
    attended, log_total = attend(windows, allowed)
    attn_tokens = from_windows(attended.reshape(-1, WIN * WIN, head_cols), slots, shifted)
    rows = attn_tokens
    middle = (
        residual
        + lax.psum_scatter(
            jnp.einsum("tsh,hd->tsd", rows, w_proj, preferred_element_type=jnp.float32).astype(
                jnp.bfloat16
            ),
            "tensor",
            scatter_dimension=0,
            tiled=True,
        ).astype(jnp.float32)
        + out_bias
    )
    normed_b, normal_b, inverse_b = layer_norm(middle, gain_b, offset_b)
    mlp_input = lax.all_gather(normed_b.astype(jnp.bfloat16), "tensor", axis=0, tiled=True)
    pre_act = (
        jnp.einsum("tsd,df->tsf", mlp_input, w_fc1, preferred_element_type=jnp.float32) + fc_bias
    )
    hidden = exact_gelu(pre_act).astype(jnp.bfloat16)
    rows = hidden
    output = (
        middle
        + lax.psum_scatter(
            jnp.einsum("tsf,fd->tsd", rows, w_fc2, preferred_element_type=jnp.float32).astype(
                jnp.bfloat16
            ),
            "tensor",
            scatter_dimension=0,
            tiled=True,
        ).astype(jnp.float32)
        + last_bias
    ).astype(jnp.bfloat16)
    saved = (
        normal_a,
        inverse_a,
        attn_input,
        windows,
        log_total,
        attn_tokens,
        normal_b,
        inverse_b,
        mlp_input,
        pre_act,
        hidden,
    )
    return (output, saved)


def layer_backward(grad, saved, matrices, vectors, shifted, allowed, tensor_index):
    w_qkv, w_proj, w_fc1, w_fc2 = matrices
    gain_a, offset_a, qkv_bias, out_bias, gain_b, offset_b, fc_bias, last_bias = vectors
    (
        normal_a,
        inverse_a,
        attn_input,
        windows,
        log_total,
        attn_tokens,
        normal_b,
        inverse_b,
        mlp_input,
        pre_act,
        hidden,
    ) = saved
    local_tokens, slots, width = grad.shape
    head_cols = w_qkv.shape[2]
    hidden_cols = w_fc1.shape[1]
    tokens = attn_input.shape[0]
    grad_full = lax.all_gather(grad.astype(jnp.bfloat16), "tensor", axis=0, tiled=True)
    grad_fc2 = jnp.einsum("tsf,tsd->fd", hidden, grad_full, preferred_element_type=jnp.float32)
    grad_hidden = jnp.einsum("tsd,fd->tsf", grad_full, w_fc2, preferred_element_type=jnp.float32)
    grad_pre = jax.vjp(exact_gelu, pre_act)[1](grad_hidden)[0]
    grad_pre_low = grad_pre.astype(jnp.bfloat16)
    grad_fc1 = jnp.einsum(
        "tsd,tsf->df", mlp_input, grad_pre_low, preferred_element_type=jnp.float32
    )
    rows = grad_pre_low
    grad_mlp_in = lax.psum_scatter(
        jnp.einsum("tsf,df->tsd", rows, w_fc1, preferred_element_type=jnp.float32).astype(
            jnp.bfloat16
        ),
        "tensor",
        scatter_dimension=0,
        tiled=True,
    ).astype(jnp.float32)
    grad_mid = grad + norm_back(grad_mlp_in, normal_b, inverse_b, gain_b)
    grad_mid_full = lax.all_gather(grad_mid.astype(jnp.bfloat16), "tensor", axis=0, tiled=True)
    grad_proj = jnp.einsum(
        "tsh,tsd->hd", attn_tokens, grad_mid_full, preferred_element_type=jnp.float32
    )
    grad_attn = jnp.einsum(
        "tsd,hd->tsh", grad_mid_full, w_proj, preferred_element_type=jnp.float32
    ).astype(jnp.bfloat16)
    grad_windows = to_windows(grad_attn, shifted).reshape(
        -1, WIN * WIN, head_cols // HEAD_DIM, HEAD_DIM
    )
    grad_query, grad_key, grad_value = attend_back(windows, log_total, grad_windows, allowed)
    stacked = jnp.stack([grad_query, grad_key, grad_value], axis=2).astype(jnp.bfloat16)
    grad_qkv_low = from_windows(stacked.reshape(-1, WIN * WIN, 3 * head_cols), slots, shifted)
    grad_qkv_low = grad_qkv_low.reshape(tokens, slots, 3, head_cols)
    grad_qkv = jnp.einsum(
        "tsd,tsch->dch", attn_input, grad_qkv_low, preferred_element_type=jnp.float32
    )
    rows = grad_qkv_low
    grad_attn_in = lax.psum_scatter(
        jnp.einsum("tsch,dch->tsd", rows, w_qkv, preferred_element_type=jnp.float32).astype(
            jnp.bfloat16
        ),
        "tensor",
        scatter_dimension=0,
        tiled=True,
    ).astype(jnp.float32)
    grad_inputs = grad_mid + norm_back(grad_attn_in, normal_a, inverse_a, gain_a)

    def place(piece, offset):
        return lax.dynamic_update_slice_in_dim(jnp.zeros((width,), jnp.float32), piece, offset, 0)

    gain_grads = jnp.stack(
        [
            jnp.sum(grad_attn_in * normal_a, axis=(0, 1)),
            jnp.sum(grad_mlp_in * normal_b, axis=(0, 1)),
        ]
    )
    bias_rows = jnp.stack(
        [
            jnp.sum(grad_attn_in, axis=(0, 1)),
            place(jnp.sum(grad_query, axis=(0, 1)).reshape(head_cols), tensor_index * head_cols),
            place(jnp.sum(grad_value, axis=(0, 1)).reshape(head_cols), tensor_index * head_cols),
            jnp.sum(grad_mid, axis=(0, 1)),
            jnp.sum(grad_mlp_in, axis=(0, 1)),
            jnp.sum(grad, axis=(0, 1)),
        ]
    )
    fc_rows = lax.dynamic_update_slice_in_dim(
        jnp.zeros((FF,), jnp.float32), jnp.sum(grad_pre, axis=(0, 1)), tensor_index * hidden_cols, 0
    )
    bias_grads = jnp.concatenate([bias_rows, fc_rows.reshape(-1, width)], axis=0)
    return (grad_inputs, ((grad_qkv, grad_proj, grad_fc1, grad_fc2), (gain_grads, bias_grads)))


def reduce_grads(terms):
    weight_parts = (
        lax.psum_scatter(
            terms[0][0].astype(jnp.bfloat16), "dp", scatter_dimension=0, tiled=True
        ).astype(jnp.float32),
        lax.psum_scatter(
            terms[0][1].astype(jnp.bfloat16), "dp", scatter_dimension=1, tiled=True
        ).astype(jnp.float32),
        lax.psum_scatter(
            terms[0][2].astype(jnp.bfloat16), "dp", scatter_dimension=0, tiled=True
        ).astype(jnp.float32),
        lax.psum_scatter(
            terms[0][3].astype(jnp.bfloat16), "dp", scatter_dimension=1, tiled=True
        ).astype(jnp.float32),
    )
    vector_parts = (
        lax.psum_scatter(terms[1][0], ("dp", "tensor"), scatter_dimension=1, tiled=True),
        lax.psum_scatter(terms[1][1], ("dp", "tensor"), scatter_dimension=1, tiled=True),
    )
    return (tuple(weight_parts), tuple(vector_parts))


def shards(boundary, live, w_qkv, w_proj, w_fc1, w_fc2, gains, biases):
    section_index = lax.axis_index("section")
    tensor_index = lax.axis_index("tensor")
    shifted = section_index == 1
    micro = boundary.shape[1]
    slots = boundary.shape[3]
    head_cols = w_qkv.shape[3]
    hidden_cols = w_fc1.shape[2]
    slot_keep = (jnp.arange(slots)[None, :] < live).astype(jnp.float32)
    allowed = region_keep(shifted, slots)

    def gather_weights():
        return (
            lax.all_gather(w_qkv[0], "dp", axis=0, tiled=True),
            lax.all_gather(w_proj[0], "dp", axis=1, tiled=True),
            lax.all_gather(w_fc1[0], "dp", axis=0, tiled=True),
            lax.all_gather(w_fc2[0], "dp", axis=1, tiled=True),
            lax.all_gather(gains[0], "dp", axis=1, tiled=True),
            lax.all_gather(biases[0], "dp", axis=1, tiled=True),
        )

    def fetch_weights():
        return gather_weights()

    def unpack(gathered):
        matrices = (gathered[0], gathered[1], gathered[2], gathered[3])
        vectors = split_vectors(gathered[4], gathered[5], tensor_index, head_cols, hidden_cols)
        return (matrices, vectors)

    arrivals = jnp.zeros_like(boundary[0, 0])
    saved_list = []
    out_list = []
    for moment in range(micro + 1):
        own_input = boundary[0, min(moment, micro - 1)]
        layer_input = jnp.where(shifted, arrivals, own_input)
        matrices, vectors = unpack(fetch_weights())
        layer_out, saved = layer_forward(layer_input, matrices, vectors, shifted, allowed)
        saved_list.append(saved)
        out_list.append(layer_out)
        if moment < micro:
            arrivals = from_behind(layer_out, "section", 1)
    arrivals_back = jnp.zeros_like(boundary[0, 0])
    grads_in = []
    collected = None
    for moment in range(micro + 1):
        later_index = min(moment, micro - 1)
        valid = 1.0 if moment < micro else 0.0
        cotangent = boundary[0, later_index].astype(jnp.float32) * (
            slot_keep[later_index][None, :, None] * valid
        )
        grad = jnp.where(shifted, cotangent, arrivals_back.astype(jnp.float32))
        saved = jax.tree.map(
            lambda later, earlier: jnp.where(shifted, later, earlier),
            saved_list[min(moment + 1, micro)],
            saved_list[max(moment - 1, 0)],
        )
        matrices, vectors = unpack(fetch_weights())
        grad_inputs, terms = layer_backward(
            grad, saved, matrices, vectors, shifted, allowed, tensor_index
        )
        grads_in.append(grad_inputs)
        if moment < micro:
            arrivals_back = from_behind(grad_inputs.astype(jnp.bfloat16), "section", -1)
        reduced = reduce_grads(terms)
        collected = reduced if collected is None else jax.tree.map(jnp.add, collected, reduced)
    outputs = jnp.stack(
        [
            out_list[index + 1].astype(jnp.float32) * slot_keep[index][None, :, None]
            for index in range(micro)
        ]
    )
    inputs_grad = jnp.stack([grads_in[index + 1] for index in range(micro)])
    results = jnp.where(shifted, outputs, inputs_grad)[None]
    weight_parts, vector_parts = collected
    return (
        results,
        weight_parts[0][None],
        weight_parts[1][None],
        weight_parts[2][None],
        weight_parts[3][None],
        vector_parts[0][None],
        vector_parts[1][None],
    )


def solution(mesh):
    placed = (
        P("section", None, "tensor", "dp", None),
        P(None, "dp"),
        P("section", "dp", None, "tensor"),
        P("section", "tensor", "dp"),
        P("section", "dp", "tensor"),
        P("section", "tensor", "dp"),
        P("section", None, "dp"),
        P("section", None, "dp"),
    )
    return jax.shard_map(
        shards,
        mesh=mesh,
        in_specs=placed,
        out_specs=(
            P("section", None, "tensor", "dp", None),
            P("section", "dp", None, "tensor"),
            P("section", "tensor", "dp"),
            P("section", "dp", "tensor"),
            P("section", "tensor", "dp"),
            P("section", None, ("dp", "tensor")),
            P("section", None, ("dp", "tensor")),
        ),
        check_vma=False,
    )
```

profile of v0, /device:TPU:0, one launch (start us, length us, event | category | flops | bytes accessed | tf_op | source)
XLA Modules:
  0.0 2838.4 jit_solution(2451353219852739448)
XLA Ops:
  108.5 53.5 %all-reduce.41.cloned.1.call-done = bf16[196,6,512]{2,0,1:T(8,128)(2,1)} async-done(((bf16[196,6,512]{2,0,1:T(8,128)(2,1)}), bf16[196,6,512]{2,0,1:T(8,128)(2,1)}) %all-reduce.41.cloned.1.call-update) | async-done | bytes 1204240
  210.2 54.9 %all-reduce.43.cloned.1.call-done = bf16[196,6,512]{2,0,1:T(8,128)(2,1)} async-done(((bf16[196,6,512]{2,0,1:T(8,128)(2,1)}), bf16[196,6,512]{2,0,1:T(8,128)(2,1)}) %all-reduce.43.cloned.1.call-update) | async-done | bytes 1204240
  272.0 31.4 %all-gather.31.cloned.1.call-done = bf16[196,6,512]{2,1,0:T(8,128)(2,1)} async-done(((bf16[49,6,512]{2,1,0:T(8,128)(2,1)}), bf16[196,6,512]{2,1,0:T(8,128)(2,1)}) %all-gather.31.cloned.1.call-update) | async-done | bytes 1204240 | tf_op jit(solution)/shard_map/all_gather | solution.py:150
  361.7 55.0 %all-reduce.45.cloned.1.call-done = bf16[196,6,512]{2,0,1:T(8,128)(2,1)} async-done(((bf16[196,6,512]{2,0,1:T(8,128)(2,1)}), bf16[196,6,512]{2,0,1:T(8,128)(2,1)}) %all-reduce.45.cloned.1.call-update) | async-done | bytes 1204240
  423.6 28.0 all-gather.33.cloned.1.call-done
  456.2 28.3 all-gather.47.cloned.1.call-done
  506.3 75.8 %all-reduce.65.cloned.1.call-done = (bf16[196,6,512]{2,0,1:T(8,128)(2,1)}, bf16[196,6,512]{2,0,1:T(8,128)(2,1)}) async-done(((bf16[196,6,512]{2,0,1:T(8,128)(2,1)}, bf16[196,6,512]{2,0,1:T(8,128)(2,1)}), (bf16[196,6,512]{2,0,1:T(8,128)(2,1)}, bf16[196,6,512]{2,0,1:T(8,128)(2,1)})) %all-reduce.65.cloned.1.call-update) | async-done | bytes 2408464
  595.1 25.9 all-gather.49.cloned.1.call-done
  775.3 76.1 %all-reduce.63.cloned.1.call-done = (bf16[196,6,512]{2,0,1:T(8,128)(2,1)}, bf16[196,6,512]{2,0,1:T(8,128)(2,1)}) async-done(((bf16[196,6,512]{2,0,1:T(8,128)(2,1)}, bf16[196,6,512]{2,0,1:T(8,128)(2,1)}), (bf16[196,6,512]{2,0,1:T(8,128)(2,1)}, bf16[196,6,512]{2,0,1:T(8,128)(2,1)})) %all-reduce.63.cloned.1.call-update) | async-done | bytes 2408464
  932.4 75.8 %all-reduce.61.cloned.1.call-done = (bf16[196,6,512]{2,0,1:T(8,128)(2,1)}, bf16[196,6,512]{2,0,1:T(8,128)(2,1)}) async-done(((bf16[196,6,512]{2,0,1:T(8,128)(2,1)}, bf16[196,6,512]{2,0,1:T(8,128)(2,1)}), (bf16[196,6,512]{2,0,1:T(8,128)(2,1)}, bf16[196,6,512]{2,0,1:T(8,128)(2,1)})) %all-reduce.61.cloned.1.call-update) | async-done | bytes 2408464
  1023.9 24.0 all-gather.53.cloned.1.call-done
  1191.9 75.8 %all-reduce.59.cloned.1.call-done = (bf16[196,6,512]{2,0,1:T(8,128)(2,1)}, bf16[196,6,512]{2,0,1:T(8,128)(2,1)}) async-done(((bf16[196,6,512]{2,0,1:T(8,128)(2,1)}, bf16[196,6,512]{2,0,1:T(8,128)(2,1)}), (bf16[196,6,512]{2,0,1:T(8,128)(2,1)}, bf16[196,6,512]{2,0,1:T(8,128)(2,1)})) %all-reduce.59.cloned.1.call-update) | async-done | bytes 2408464
  1351.3 75.8 %all-reduce.57.cloned.1.call-done = (bf16[196,6,512]{2,0,1:T(8,128)(2,1)}, bf16[196,6,512]{2,0,1:T(8,128)(2,1)}) async-done(((bf16[196,6,512]{2,0,1:T(8,128)(2,1)}, bf16[196,6,512]{2,0,1:T(8,128)(2,1)}), (bf16[196,6,512]{2,0,1:T(8,128)(2,1)}, bf16[196,6,512]{2,0,1:T(8,128)(2,1)})) %all-reduce.57.cloned.1.call-update) | async-done | bytes 2408464
  1440.9 26.0 all-gather.57.cloned.1.call-done
  1630.7 75.4 %all-reduce.55.cloned.1.call-done = (bf16[196,6,512]{2,0,1:T(8,128)(2,1)}, bf16[196,6,512]{2,0,1:T(8,128)(2,1)}) async-done(((bf16[196,6,512]{2,0,1:T(8,128)(2,1)}, bf16[196,6,512]{2,0,1:T(8,128)(2,1)}), (bf16[196,6,512]{2,0,1:T(8,128)(2,1)}, bf16[196,6,512]{2,0,1:T(8,128)(2,1)})) %all-reduce.55.cloned.1.call-update) | async-done | bytes 2408464
  1748.1 27.4 all-gather.59.cloned.1.call-done
  1788.7 55.2 %all-reduce.47.cloned.1.call-done = bf16[196,6,512]{2,0,1:T(8,128)(2,1)} async-done(((bf16[196,6,512]{2,0,1:T(8,128)(2,1)}), bf16[196,6,512]{2,0,1:T(8,128)(2,1)}) %all-reduce.47.cloned.1.call-update) | async-done | bytes 1204240
  1854.7 27.5 all-gather.61.cloned.1.call-done
  1959.6 55.2 %all-reduce.49.cloned.1.call-done = bf16[196,6,512]{2,0,1:T(8,128)(2,1)} async-done(((bf16[196,6,512]{2,0,1:T(8,128)(2,1)}), bf16[196,6,512]{2,0,1:T(8,128)(2,1)}) %all-reduce.49.cloned.1.call-update) | async-done | bytes 1204240
  2024.6 31.4 %all-gather.63.cloned.1.call-done = bf16[196,6,512]{2,1,0:T(8,128)(2,1)} async-done(((bf16[49,6,512]{2,1,0:T(8,128)(2,1)}), bf16[196,6,512]{2,1,0:T(8,128)(2,1)}) %all-gather.63.cloned.1.call-update) | async-done | bytes 1204240 | tf_op jit(solution)/shard_map/all_gather | solution.py:230
  2070.8 55.2 %all-reduce.51.cloned.1.call-done = bf16[196,6,512]{2,0,1:T(8,128)(2,1)} async-done(((bf16[196,6,512]{2,0,1:T(8,128)(2,1)}), bf16[196,6,512]{2,0,1:T(8,128)(2,1)}) %all-reduce.51.cloned.1.call-update) | async-done | bytes 1204240
  2598.4 75.8 %all-reduce.53.cloned.1.call-done = (bf16[196,6,512]{2,0,1:T(8,128)(2,1)}, bf16[196,6,512]{2,0,1:T(8,128)(2,1)}) async-done(((bf16[196,6,512]{2,0,1:T(8,128)(2,1)}, bf16[196,6,512]{2,0,1:T(8,128)(2,1)}), (bf16[196,6,512]{2,0,1:T(8,128)(2,1)}, bf16[196,6,512]{2,0,1:T(8,128)(2,1)})) %all-reduce.53.cloned.1.call-update) | async-done | bytes 2408464
  2686.4 67.9 %reduce-scatter.107.cloned.1.call-done = f32[32,2]{1,0:T(8,128)} async-done(((f32[512,2]{1,0:T(8,128)}), f32[32,2]{1,0:T(8,128)}) %reduce-scatter.107.cloned.1.call-update) | async-done | bytes 272
  2755.7 74.3 %reduce-scatter.109.cloned.1.call-done = f32[32,10]{1,0:T(8,128)} async-done(((f32[512,10]{1,0:T(8,128)}), f32[32,10]{1,0:T(8,128)}) %reduce-scatter.109.cloned.1.call-update) | async-done | bytes 1296
  (1320 shorter events, 1566.9 us)
Async XLA Ops:
  423.5 158.6 %all-reduce.65.cloned.1.call-start = ((), (), s32[]{:S(2)}) async-start(), calls=%async_computation.76 | async-start | bytes 4915200
  595.0 256.4 %all-reduce.63.cloned.1.call-start = ((), (), s32[]{:S(2)}) async-start(), calls=%async_computation.75 | async-start | bytes 4915200
  1023.8 243.8 %all-reduce.59.cloned.1.call-start = ((), (), s32[]{:S(2)}) async-start(), calls=%async_computation.73 | async-start | bytes 4915200
  1440.9 265.2 %all-reduce.55.cloned.1.call-start = ((), (), s32[]{:S(2)}) async-start(), calls=%async_computation.71 | async-start | bytes 4915200
  1850.9 164.0 %all-reduce.49.cloned.1.call-start = ((), (), s32[]{:S(2)}) async-start(), calls=%async_computation.68 | async-start | bytes 2457600
  2133.4 171.6 %reduce-scatter.97.cloned.1.call-start = ((), (), s32[]{:S(2)}) async-start(), calls=%async_computation.57 | async-start | bytes 655360
  2139.6 166.5 %reduce-scatter.87.cloned.1.call-start = ((), (), s32[]{:S(2)}) async-start(), calls=%async_computation.52 | async-start | bytes 163840
  2142.9 164.7 %reduce-scatter.99.cloned.1.call-start = ((), (), s32[]{:S(2)}) async-start(), calls=%async_computation.58 | async-start | bytes 655360
  2149.0 159.9 %reduce-scatter.89.cloned.1.call-start = ((), (), s32[]{:S(2)}) async-start(), calls=%async_computation.53 | async-start | bytes 163840
  2176.1 160.3 %reduce-scatter.93.cloned.1.call-start = ((), (), s32[]{:S(2)}) async-start(), calls=%async_computation.55 | async-start | bytes 163840
  2179.3 179.4 %reduce-scatter.105.cloned.1.call-start = ((), (), s32[]{:S(2)}) async-start(), calls=%async_computation.61 | async-start | bytes 655360
  2185.4 195.7 %reduce-scatter.77.cloned.1.call-start = ((), (), s32[]{:S(2)}) async-start(), calls=%async_computation.47 | async-start | bytes 655360 | tf_op jit(solution)/shard_map/reduce_scatter | solution.py:310
  2190.4 212.9 %reduce-scatter.79.cloned.1.call-start = ((), (), s32[]{:S(2)}) async-start(), calls=%async_computation.48 | async-start | bytes 655360 | tf_op jit(solution)/shard_map/reduce_scatter | solution.py:310
  2195.4 230.4 %reduce-scatter.81.cloned.1.call-start = ((), (), s32[]{:S(2)}) async-start(), calls=%async_computation.49 | async-start | bytes 655360 | tf_op jit(solution)/shard_map/reduce_scatter | solution.py:310
  2200.5 247.5 %reduce-scatter.83.cloned.1.call-start = ((), (), s32[]{:S(2)}) async-start(), calls=%async_computation.50 | async-start | bytes 655360 | tf_op jit(solution)/shard_map/reduce_scatter | solution.py:310
  2205.5 264.8 %reduce-scatter.85.cloned.1.call-start = ((), (), s32[]{:S(2)}) async-start(), calls=%async_computation.51 | async-start | bytes 655360 | tf_op jit(solution)/shard_map/reduce_scatter | solution.py:310
  2210.5 280.2 %reduce-scatter.95.cloned.1.call-start = ((), (), s32[]{:S(2)}) async-start(), calls=%async_computation.56 | async-start | bytes 163840
  2213.7 298.0 %reduce-scatter.67.cloned.1.call-start = ((), (), s32[]{:S(2)}) async-start(), calls=%async_computation.42 | async-start | bytes 491520 | tf_op jit(solution)/shard_map/reduce_scatter | solution.py:304
  2219.2 313.7 %reduce-scatter.69.cloned.1.call-start = ((), (), s32[]{:S(2)}) async-start(), calls=%async_computation.43 | async-start | bytes 491520 | tf_op jit(solution)/shard_map/reduce_scatter | solution.py:304
  2224.6 329.6 %reduce-scatter.71.cloned.1.call-start = ((), (), s32[]{:S(2)}) async-start(), calls=%async_computation.44 | async-start | bytes 491520 | tf_op jit(solution)/shard_map/reduce_scatter | solution.py:304
  2229.9 345.4 %reduce-scatter.73.cloned.1.call-start = ((), (), s32[]{:S(2)}) async-start(), calls=%async_computation.45 | async-start | bytes 491520 | tf_op jit(solution)/shard_map/reduce_scatter | solution.py:304
  2237.5 359.1 %reduce-scatter.75.cloned.1.call-start = ((), (), s32[]{:S(2)}) async-start(), calls=%async_computation.46 | async-start | bytes 491520 | tf_op jit(solution)/shard_map/reduce_scatter | solution.py:304
  2299.4 374.8 %all-reduce.53.cloned.1.call-start = ((), (), s32[]{:S(2)}) async-start(), calls=%async_computation.70 | async-start | bytes 4915200
  2304.6 449.7 %reduce-scatter.107.cloned.1.call-start = ((), (), s32[]{:S(2)}) async-start(), calls=%async_computation.62 | async-start | bytes 278528
  (310 other events, 17982.7 us)
Sparse Core Ops, SparseCore 0:
  106.8 55.0 all-reduce.40
  164.9 31.2 all-gather.28
  210.3 54.7 all-reduce.42
  272.1 31.2 all-gather.30
  361.6 55.1 all-reduce.44
  420.3 31.2 all-gather.32
  506.4 75.6 all-reduce.64
  774.9 76.3 all-reduce.62
  887.7 31.1 all-gather.50
  932.5 75.6 all-reduce.60
  1016.8 31.0 all-gather.52
  1192.0 75.6 all-reduce.58
  1351.4 75.6 all-reduce.56
  1630.4 75.6 all-reduce.54
  1744.4 31.0 all-gather.58
  1788.8 55.0 all-reduce.46
  1851.0 31.2 all-gather.60
  1959.6 55.1 all-reduce.48
  2024.7 31.2 all-gather.62
  2070.8 55.0 all-reduce.50
  2133.5 31.2 all-gather.64
  2600.2 73.9 all-reduce.52
  2677.2 77.0 reduce-scatter.106
  2756.6 73.3 reduce-scatter.108
  (31 shorter events, 724.5 us)
where the time goes:
time: 2850 us; the launch traced here: 2840 us
  waiting for transfers between devices  1680 us (59%)
  local copies, waits for them, and re-layouts  517 us (18%)
  matrix products  344 us (12%)
  other arithmetic  176 us (6%)
  blocking collectives  83.9 us (3%)
    unnamed x80, waiting for transfers between devices  1060 us
    all_gather x5, waiting for transfers between devices, layer_backward(): lax.all_gather(grad.astype(jnp.bfloat16), 'tensor', axis=0, tiled=True)  125 us
    reduce_scatter x5, waiting for transfers between devices, reduce_grads(): lax.psum_scatter(terms[0][2].astype(jnp.bfloat16), 'dp', scatter_dimensio...  110 us
    reduce_scatter x5, waiting for transfers between devices, reduce_grads(): lax.psum_scatter(terms[0][0].astype(jnp.bfloat16), 'dp', scatter_dimensio...  104 us
    all_gather x5, waiting for transfers between devices, layer_backward(): lax.all_gather(grad_mid.astype(jnp.bfloat16), 'tensor', axis=0, tiled=True)  103 us
    unnamed x587, local copies, waits for them, and re-layouts  98.4 us
    all_gather x5, waiting for transfers between devices, layer_forward(): lax.all_gather(normed_b.astype(jnp.bfloat16), 'tensor', axis=0, tiled=True)  90.7 us
    all_gather x5, waiting for transfers between devices, layer_forward(): lax.all_gather(normed.astype(jnp.bfloat16), 'tensor', axis=0, tiled=True)  71.4 us
  transfers between devices with their start and end apart: 63, of which 53 were waited for; matrix products, arithmetic and copies ran while one was open for 13% of the time, Pallas kernels for 0%

commit v1 on v0

v1 whole, which is shorter than its diff:
```python
import functools

import jax
import jax.numpy as jnp
import numpy as np
from jax import lax
from jax.experimental import pallas as pl
from jax.experimental.pallas import tpu as pltpu
from jax.sharding import PartitionSpec as P

HEAD_DIM = 32
GRID = 14
WIN = 7
SHIFT = 3
EPSILON = 1e-05
TOK = GRID * GRID
D = 512
PAD = 64
IMG = 4 * PAD
GROUP = 8
SCALE = HEAD_DIM ** (-0.5)
F32 = jnp.float32
BF16 = jnp.bfloat16
LIMIT = 60 * 1024 * 1024

ANY = pl.BlockSpec(memory_space=pl.ANY)
VM = pl.BlockSpec(memory_space=pltpu.VMEM)
SM = pl.BlockSpec(memory_space=pltpu.SMEM)


def token_of(shifted):
    rows = -np.ones((IMG,), np.int64)
    for window in range(4):
        for r in range(WIN * WIN):
            row = (window // 2) * WIN + r // WIN
            col = (window % 2) * WIN + r % WIN
            if shifted:
                row, col = (row + SHIFT) % GRID, (col + SHIFT) % GRID
            rows[window * PAD + r] = row * GRID + col
    return rows


def one_hot(rows):
    return (rows[:, None] == np.arange(TOK)[None, :]).astype(np.float32)


def dot(a, b, ca=1, cb=0):
    return lax.dot_general(a, b, (((ca,), (cb,)), ((), ())), preferred_element_type=F32)


def normalize(values):
    centred = values - jnp.mean(values, axis=-1, keepdims=True)
    inverse = lax.rsqrt(jnp.mean(centred * centred, axis=-1, keepdims=True) + EPSILON)
    return centred * inverse, inverse


def norm_back(grad, normal, inverse, gain):
    scaled = grad * gain
    return inverse * (
        scaled
        - jnp.mean(scaled, axis=-1, keepdims=True)
        - normal * jnp.mean(scaled * normal, axis=-1, keepdims=True)
    )


def iota(shape, dim):
    return lax.broadcasted_iota(jnp.int32, shape, dim)


def shr(values, by):
    return lax.shift_right_logical(values, jnp.int32(by))


def head_mask():
    shape = (GROUP * PAD, GROUP * HEAD_DIM)
    return jnp.where(shr(iota(shape, 0), 6) == shr(iota(shape, 1), 5), 1.0, 0.0).astype(BF16)


def block_ones():
    shape = (GROUP * PAD, GROUP * PAD)
    return jnp.where(shr(iota(shape, 0), 6) == shr(iota(shape, 1), 6), 1.0, 0.0).astype(BF16)


def head_ones():
    shape = (GROUP * HEAD_DIM, GROUP * PAD)
    return jnp.where(shr(iota(shape, 0), 5) == shr(iota(shape, 1), 6), 1.0, 0.0).astype(BF16)


def allowed_pairs(window, shifted):
    shape = (PAD, GROUP * PAD)
    query, key = iota(shape, 0), iota(shape, 1) & (PAD - 1)
    allowed = key < WIN * WIN
    if shifted:
        query_row, key_row = shr(query * 37, 8), shr(key * 37, 8)
        query_col, key_col = query - WIN * query_row, key - WIN * key_row
        edge = WIN - SHIFT
        rows = (query_row >= edge) == (key_row >= edge)
        cols = (query_col >= edge) == (key_col >= edge)
        if window // 2 == 1:
            allowed = allowed & rows
        if window % 2 == 1:
            allowed = allowed & cols
    return jnp.where(allowed, 1.0, 0.0).astype(F32)


def spread(rows, mask):
    return jnp.concatenate([rows] * GROUP, axis=0) * mask


def fold(full, mask):
    full = full * mask
    total = full[0:PAD]
    for head in range(1, GROUP):
        total = total + full[head * PAD : (head + 1) * PAD]
    return total


def load_attn_weights(layer, gathered, w_qkv, w_proj, sem):
    copies = []
    height = gathered.shape[1]
    parts = D // height
    for j in range(parts):
        for t in range(4):
            block = gathered.at[(layer * parts + j) * 4 + t]
            rows = pl.ds(j * height, height)
            for c in range(3):
                copies.append((block.at[:, pl.ds(c * 128, 128)], w_qkv.at[rows, pl.ds(c * D + t * 128, 128)]))
            copies.append((block.at[:, pl.ds(384, 128)], w_proj.at[rows, pl.ds(t * 128, 128)]))
    return [pltpu.make_async_copy(src, dst, sem) for src, dst in copies]


def load_mlp_weights(layer, gathered, w_fc1, w_fc2, sem):
    copies = []
    height = gathered.shape[1] // 2
    parts = D // height
    for j in range(parts):
        for t in range(4):
            block = gathered.at[(layer * parts + j) * 4 + t]
            rows, cols = pl.ds(j * height, height), pl.ds(t * D, D)
            copies.append((block.at[pl.ds(0, height)], w_fc1.at[rows, cols]))
            copies.append((block.at[pl.ds(height, height)], w_fc2.at[rows, cols]))
    return [pltpu.make_async_copy(src, dst, sem) for src, dst in copies]


def each(count, body):
    def step(index, carry):
        body(index)
        return carry

    lax.fori_loop(0, count, step, 0)


def image_rows(index):
    return pl.ds(pl.multiple_of(index * IMG, IMG), IMG)


def attn_forward_kernel(
    layer, images, source, perm, vec, gathered,
    x_out, a_out, qkv_out, p_out, attn_out, mid_out,
    w_qkv, w_proj, mask, ones, pairs, sem,
):
    copies = load_attn_weights(layer, gathered, w_qkv, w_proj, sem)
    for copy in copies:
        copy.start()
    mask[...] = head_mask()
    ones[...] = block_ones()
    for window in range(4):
        pairs[window] = allowed_pairs(window, layer == 1)
    for copy in copies:
        copy.wait()
    gain, offset = vec[0:1], vec[2:3]
    query_bias, value_bias, out_bias = vec[3:4], vec[4:5], vec[5:6]

    def one_image(i):
        rows = image_rows(i)
        if layer == 0:
            x = dot(perm[0], source[0, i])
            for t in range(1, 4):
                x = x + dot(perm[t], source[t, i])
        else:
            x = dot(perm[...], source[rows])
        x_out[rows] = x.astype(BF16)
        normal, _ = normalize(x)
        a = (normal * gain + offset).astype(BF16)
        a_out[rows] = a
        qkv_out[rows, 0:D] = (dot(a, w_qkv[:, 0:D]) + query_bias).astype(BF16)
        qkv_out[rows, D : 2 * D] = dot(a, w_qkv[:, D : 2 * D]).astype(BF16)
        qkv_out[rows, 2 * D : 3 * D] = (dot(a, w_qkv[:, 2 * D : 3 * D]) + value_bias).astype(BF16)

        def one_window(w):
            own = pl.ds(pl.multiple_of(i * IMG + w * PAD, PAD), PAD)
            for g in range(2):
                low, high = g * 256, (g + 1) * 256
                q = qkv_out[own, low:high]
                k = spread(qkv_out[own, D + low : D + high], mask[...])
                v = spread(qkv_out[own, 2 * D + low : 2 * D + high], mask[...])
                weights = jnp.exp(dot(q, k, 1, 1) * SCALE) * pairs[w]
                total = dot(weights.astype(BF16), ones[...])
                probs = (weights / total).astype(BF16)
                p_out[i * 4 + w, g] = probs
                attn_out[own, low:high] = dot(probs, v).astype(BF16)

        each(4, one_window)
        mid_out[rows] = x + dot(attn_out[rows], w_proj[...], 1, 1) + out_bias

    each(images, one_image)


def mlp_forward_kernel(
    layer, images, keep, mid, perm, vec, gathered,
    m_out, hidden_out, slope_out, final_out,
    w_fc1, w_fc2, acc, sem,
):
    copies = load_mlp_weights(layer, gathered, w_fc1, w_fc2, sem)
    for copy in copies:
        copy.start()
    for copy in copies:
        copy.wait()
    gain, offset, last_bias = vec[1:2], vec[6:7], vec[7:8]

    def one_image(i):
        rows = image_rows(i)
        normal, _ = normalize(mid[rows])
        m_out[rows] = (normal * gain + offset).astype(BF16)
        acc[...] = mid[rows] + last_bias

        def one_chunk(f):
            cols = pl.ds(pl.multiple_of(f * D, D), D)
            pre = dot(m_out[rows], w_fc1[:, cols]) + vec[pl.ds(8 + f, 1)]
            cdf = 0.5 + 0.5 * lax.erf(pre * np.float32(np.sqrt(0.5)))
            density = jnp.exp(-0.5 * pre * pre) * np.float32(1.0 / np.sqrt(2 * np.pi))
            hidden = (pre * cdf).astype(BF16)
            hidden_out[rows, cols] = hidden
            slope_out[rows, cols] = (cdf + pre * density).astype(BF16)
            acc[...] += dot(hidden, w_fc2[:, cols], 1, 1)

        each(4, one_chunk)
        out = acc[...].astype(BF16)
        if layer == 0:
            final_out[rows] = out
        else:
            for t in range(4):
                final_out[t, i] = (dot(perm[t], out) * keep[i]).astype(BF16)

    each(images, one_image)


def mlp_backward_kernel(
    layer, images, keep, source, perm, mid, m_in, hidden, slope, vec, gathered,
    mid_grad, block_out, sums,
    w_fc1, w_fc2, gz, pre_low, acc, sem,
):
    copies = load_mlp_weights(layer, gathered, w_fc1, w_fc2, sem)
    for copy in copies:
        copy.start()
    sums[...] = jnp.zeros_like(sums)
    for copy in copies:
        copy.wait()
    gain = vec[1:2]

    def one_image(i):
        rows = image_rows(i)
        if layer == 1:
            g = dot(perm[0], source[0, i])
            for t in range(1, 4):
                g = g + dot(perm[t], source[t, i])
            g = g * keep[i]
        else:
            g = dot(perm[...], source[rows])
        gz[rows] = g.astype(BF16)
        acc[...] = jnp.zeros_like(acc)

        def one_chunk(f):
            cols = pl.ds(pl.multiple_of(f * D, D), D)
            grad_pre = dot(gz[rows], w_fc2[:, cols]) * slope[rows, cols].astype(F32)
            sums[pl.ds(8 + f, 1)] += jnp.sum(grad_pre, axis=0, keepdims=True)
            low = grad_pre.astype(BF16)
            pre_low[rows, cols] = low
            acc[...] += dot(low, w_fc1[:, cols], 1, 1)

        each(4, one_chunk)
        grad_in = acc[...]
        normal, inverse = normalize(mid[rows])
        g = gz[rows].astype(F32)
        grad_mid = g + norm_back(grad_in, normal, inverse, gain)
        mid_grad[rows] = grad_mid
        sums[1:2] += jnp.sum(grad_in * normal, axis=0, keepdims=True)
        sums[6:7] += jnp.sum(grad_in, axis=0, keepdims=True)
        sums[7:8] += jnp.sum(g, axis=0, keepdims=True)
        sums[5:6] += jnp.sum(grad_mid, axis=0, keepdims=True)

    each(images, one_image)

    def one_block(f):
        cols = pl.ds(pl.multiple_of(f * D, D), D)
        first = dot(m_in[...], pre_low[:, cols], 0, 0).astype(BF16)
        second = dot(gz[...], hidden[:, cols], 0, 0).astype(BF16)
        height = block_out.shape[1] // 2
        for j in range(D // height):
            block_out[j * 4 + f, 0:height] = first[j * height : (j + 1) * height]
            block_out[j * 4 + f, height : 2 * height] = second[j * height : (j + 1) * height]

    each(4, one_block)


def attn_backward_kernel(
    layer, images, mid_grad, x_in, a_in, qkv, p_in, attn, perm, vec, gathered,
    final_out, block_out, sums,
    w_qkv, w_proj, mask, spread_ones, gy, grad_attn, grad_qkv, sem,
):
    copies = load_attn_weights(layer, gathered, w_qkv, w_proj, sem)
    for copy in copies:
        copy.start()
    mask[...] = head_mask()
    spread_ones[...] = head_ones()
    sums[...] = jnp.zeros_like(sums)
    for copy in copies:
        copy.wait()
    gain = vec[0:1]

    def one_image(i):
        rows = image_rows(i)
        gy[rows] = mid_grad[rows].astype(BF16)
        grad_attn[...] = dot(gy[rows], w_proj[...]).astype(BF16)

        def one_window(w):
            own = pl.ds(pl.multiple_of(i * IMG + w * PAD, PAD), PAD)
            inner = pl.ds(pl.multiple_of(w * PAD, PAD), PAD)
            for g in range(2):
                low, high = g * 256, (g + 1) * 256
                q = qkv[own, low:high]
                k = spread(qkv[own, D + low : D + high], mask[...])
                v = spread(qkv[own, 2 * D + low : 2 * D + high], mask[...])
                out_grad = grad_attn[inner, low:high]
                probs = p_in[i * 4 + w, g]
                weighted = out_grad.astype(F32) * attn[own, low:high].astype(F32)
                centre = dot(weighted.astype(BF16), spread_ones[...])
                probs_grad = dot(out_grad, v, 1, 1)
                scores_grad = (probs.astype(F32) * (probs_grad - centre) * SCALE).astype(BF16)
                grad_query = dot(scores_grad, k)
                keep_mask = mask[...].astype(F32)
                grad_key = fold(dot(scores_grad, q, 0, 0), keep_mask)
                grad_value = fold(dot(probs, out_grad, 0, 0), keep_mask)
                sums[3:4, low:high] += jnp.sum(grad_query, axis=0, keepdims=True)
                sums[4:5, low:high] += jnp.sum(grad_value, axis=0, keepdims=True)
                grad_qkv[own, low:high] = grad_query.astype(BF16)
                grad_qkv[own, D + low : D + high] = grad_key.astype(BF16)
                grad_qkv[own, 2 * D + low : 2 * D + high] = grad_value.astype(BF16)

        each(4, one_window)
        grad_in = dot(grad_qkv[rows], w_qkv[...], 1, 1)
        normal, inverse = normalize(x_in[rows].astype(F32))
        grad_x = (mid_grad[rows] + norm_back(grad_in, normal, inverse, gain)).astype(BF16)
        sums[0:1] += jnp.sum(grad_in * normal, axis=0, keepdims=True)
        sums[2:3] += jnp.sum(grad_in, axis=0, keepdims=True)
        if layer == 1:
            final_out[rows] = grad_x
        else:
            for t in range(4):
                final_out[t, i] = dot(perm[t], grad_x).astype(BF16)

    each(images, one_image)
    height = block_out.shape[1]
    for c in range(4):
        if c < 3:
            full = dot(a_in[...], grad_qkv[:, c * D : (c + 1) * D], 0, 0).astype(BF16)
        else:
            full = dot(gy[...], attn[...], 0, 0).astype(BF16)
        for j in range(D // height):
            for t in range(4):
                block_out[j * 4 + t, :, c * 128 : (c + 1) * 128] = full[
                    j * height : (j + 1) * height, t * 128 : (t + 1) * 128
                ]


def shape(dims, dtype=BF16):
    return jax.ShapeDtypeStruct(dims, dtype)


def block_shape(gathered):
    return shape((gathered.shape[0] // 2,) + gathered.shape[1:])


def call(kernel, name, in_specs, outs, scratch, flops, moved):
    return pl.pallas_call(
        kernel,
        name=name,
        in_specs=in_specs,
        out_specs=[VM] * len(outs),
        out_shape=outs,
        scratch_shapes=scratch,
        compiler_params=pltpu.CompilerParams(vmem_limit_bytes=LIMIT),
        cost_estimate=pl.CostEstimate(flops=flops, bytes_accessed=moved, transcendentals=0),
    )


def attn_forward(layer, images, source, perm, vec, gathered):
    rows = images * IMG
    return call(
        functools.partial(attn_forward_kernel, layer, images),
        f"attn_forward_{layer}",
        [VM, VM, VM, ANY],
        [
            shape((rows, D)), shape((rows, D)), shape((rows, 3 * D)),
            shape((images * 4, 2, PAD, GROUP * PAD)), shape((rows, D)), shape((rows, D), F32),
        ],
        [
            pltpu.VMEM((D, 3 * D), BF16), pltpu.VMEM((D, D), BF16),
            pltpu.VMEM((GROUP * PAD, 256), BF16), pltpu.VMEM((GROUP * PAD, GROUP * PAD), BF16),
            pltpu.VMEM((4, PAD, GROUP * PAD), F32), pltpu.SemaphoreType.DMA,
        ],
        2 * rows * D * 4 * D * 3, 12 << 20,
    )(source, perm, vec, gathered)


def mlp_forward(layer, images, keep, mid, perm, vec, gathered):
    rows = images * IMG
    final = shape((rows, D)) if layer == 0 else shape((4, images, TOK // 4, D))
    return call(
        functools.partial(mlp_forward_kernel, layer, images),
        f"mlp_forward_{layer}",
        [SM, VM, VM, VM, ANY],
        [shape((rows, D)), shape((rows, 4 * D)), shape((rows, 4 * D)), final],
        [
            pltpu.VMEM((D, 4 * D), BF16), pltpu.VMEM((D, 4 * D), BF16),
            pltpu.VMEM((IMG, D), F32), pltpu.SemaphoreType.DMA,
        ],
        2 * rows * D * 8 * D * 3, 14 << 20,
    )(keep, mid, perm, vec, gathered)


def mlp_backward(layer, images, keep, source, perm, mid, m_in, hidden, slope, vec, gathered):
    rows = images * IMG
    return call(
        functools.partial(mlp_backward_kernel, layer, images),
        f"mlp_backward_{layer}",
        [SM] + [VM] * 7 + [ANY],
        [shape((rows, D), F32), block_shape(gathered), shape((16, D), F32)],
        [
            pltpu.VMEM((D, 4 * D), BF16), pltpu.VMEM((D, 4 * D), BF16),
            pltpu.VMEM((rows, D), BF16), pltpu.VMEM((rows, 4 * D), BF16),
            pltpu.VMEM((IMG, D), F32), pltpu.SemaphoreType.DMA,
        ],
        2 * rows * D * 16 * D * 2, 20 << 20,
    )(keep, source, perm, mid, m_in, hidden, slope, vec, gathered)


def attn_backward(layer, images, mid_grad, x_in, a_in, qkv, p_in, attn, perm, vec, gathered):
    rows = images * IMG
    final = shape((rows, D)) if layer == 1 else shape((4, images, TOK // 4, D))
    return call(
        functools.partial(attn_backward_kernel, layer, images),
        f"attn_backward_{layer}",
        [VM] * 8 + [ANY],
        [final, block_shape(gathered), shape((16, D), F32)],
        [
            pltpu.VMEM((D, 3 * D), BF16), pltpu.VMEM((D, D), BF16),
            pltpu.VMEM((GROUP * PAD, 256), BF16), pltpu.VMEM((256, GROUP * PAD), BF16),
            pltpu.VMEM((rows, D), BF16), pltpu.VMEM((IMG, D), BF16), pltpu.VMEM((rows, 3 * D), BF16),
            pltpu.SemaphoreType.DMA,
        ],
        2 * rows * D * 8 * D * 4, 16 << 20,
    )(mid_grad, x_in, a_in, qkv, p_in, attn, perm, vec, gathered)


def permutations():
    plain, rolled = one_hot(token_of(False)), one_hot(token_of(True))
    quarter = TOK // 4

    def pieces(matrix):
        return jnp.asarray(matrix.reshape(IMG, 4, quarter).transpose(1, 0, 2), BF16)

    def back(matrix):
        return jnp.asarray(matrix.reshape(IMG, 4, quarter).transpose(1, 2, 0), BF16)

    step = rolled @ plain.T
    return pieces(plain), back(plain), pieces(rolled), back(rolled), jnp.asarray(step, BF16), jnp.asarray(step.T, BF16)


def compute(x_in, cot_in, keep, vec, attn_w, mlp_w):
    images = x_in.shape[1]
    plain, plain_back, rolled, rolled_back, step, step_back = permutations()
    x0, a0, qkv0, p0, attn0, mid0 = attn_forward(0, images, x_in, plain, vec[0], attn_w)
    m0, hid0, slope0, h = mlp_forward(0, images, keep, mid0, step, vec[0], mlp_w)
    x1, a1, qkv1, p1, attn1, mid1 = attn_forward(1, images, h, step, vec[1], attn_w)
    m1, hid1, slope1, out = mlp_forward(1, images, keep, mid1, rolled_back, vec[1], mlp_w)
    gmid1, gm1, s_m1 = mlp_backward(1, images, keep, cot_in, rolled, mid1, m1, hid1, slope1, vec[1], mlp_w)
    cross, ga1, s_a1 = attn_backward(1, images, gmid1, x1, a1, qkv1, p1, attn1, step, vec[1], attn_w)
    gmid0, gm0, s_m0 = mlp_backward(0, images, keep, cross, step_back, mid0, m0, hid0, slope0, vec[0], mlp_w)
    grad_x, ga0, s_a0 = attn_backward(0, images, gmid0, x0, a0, qkv0, p0, attn0, plain_back, vec[0], attn_w)
    return out, grad_x, (ga0, ga1), (gm0, gm1), (s_a0 + s_m0, s_a1 + s_m1)


def shards(boundary, live, w_qkv, w_proj, w_fc1, w_fc2, gains, biases):
    everyone = ("section", "dp", "tensor")
    section = lax.axis_index("section")
    tensor = lax.axis_index("tensor")
    micro, quarter, slots = boundary.shape[1:4]
    images = slots // 2
    n_dp = lax.axis_size("dp")
    own = boundary[0].reshape(micro, quarter, 2, images, D).transpose(2, 0, 3, 1, 4)
    own = own.reshape(2 * micro, images, quarter, D)
    taken = lax.all_to_all(own, ("section", "tensor"), 0, 0, tiled=True)
    x_in, cot_in = taken[:micro], taken[micro:]
    mine = lax.dynamic_index_in_dim(live, tensor, 0, keepdims=False)[0]
    keep = (section * images + jnp.arange(images) < mine).astype(F32)

    attn_shard = jnp.concatenate([w_qkv[0].reshape(-1, 384), w_proj[0].T], axis=1)
    mlp_shard = jnp.concatenate([w_fc1[0], w_fc2[0].T], axis=0)
    attn_w = lax.all_gather(attn_shard, everyone, axis=0, tiled=False)
    mlp_w = lax.all_gather(mlp_shard, everyone, axis=0, tiled=False)
    small = jnp.concatenate([gains[0], biases[0], jnp.zeros((4, gains.shape[2]), BF16)], axis=0)
    vec = lax.all_gather(small, ("section", "dp"), axis=0, tiled=False)
    vec = vec.reshape(2, n_dp, 16, -1).transpose(0, 2, 1, 3).reshape(2, 16, D).astype(F32)

    out, grad_x, ga, gm, sums = compute(x_in, cot_in, keep, vec, attn_w, mlp_w)

    ga = lax.psum_scatter(jnp.concatenate(ga, axis=0), everyone, scatter_dimension=0, tiled=True)[0]
    gm = lax.psum_scatter(jnp.concatenate(gm, axis=0), everyone, scatter_dimension=0, tiled=True)[0]
    ga, gm = ga.astype(F32), gm.astype(F32)
    sums = jnp.stack(sums)[:, :12].reshape(2, 12, -1, D // (lax.axis_size("dp") * lax.axis_size("tensor")))
    sums = sums.transpose(0, 2, 1, 3)
    sums = lax.psum_scatter(sums.reshape((-1,) + sums.shape[2:]), everyone, scatter_dimension=0, tiled=True)[0]

    back = lax.all_to_all(
        jnp.concatenate([grad_x, out], axis=0), ("section", "tensor"), 0, 0, tiled=True
    )
    back = back.reshape(2, micro, images, quarter, D).transpose(1, 3, 0, 2, 4)
    results = back.reshape(micro, quarter, slots, D).astype(F32)
    return (
        results[None],
        ga[:, :384].reshape(1, -1, 3, 128),
        ga[:, 384:].T[None],
        gm[None, : D // n_dp],
        gm[D // n_dp :].T[None],
        sums[None, :2],
        sums[None, 2:],
    )


def solution(mesh):
    return jax.shard_map(
        shards,
        mesh=mesh,
        in_specs=(
            P("section", None, "tensor", "dp", None),
            P(None, "dp"),
            P("section", "dp", None, "tensor"),
            P("section", "tensor", "dp"),
            P("section", "dp", "tensor"),
            P("section", "tensor", "dp"),
            P("section", None, "dp"),
            P("section", None, "dp"),
        ),
        out_specs=(
            P("section", None, "tensor", "dp", None),
            P("section", "dp", None, "tensor"),
            P("section", "tensor", "dp"),
            P("section", "dp", "tensor"),
            P("section", "tensor", "dp"),
            P("section", None, ("dp", "tensor")),
            P("section", None, ("dp", "tensor")),
        ),
        check_vma=False,
    )
```

time: 2850 us -> 812 us (0.28)
  waiting for transfers between devices: 1680 us -> 543 us
  local copies, waits for them, and re-layouts: 517 us -> 37.3 us
  matrix products: 344 us -> 0 us
  Pallas kernels: 0 us -> 162 us
  other arithmetic: 176 us -> 20.7 us
  blocking collectives: 83.9 us -> 24.1 us
    unnamed x80 -> x5, waiting for transfers between devices: 1060 us -> 0.08 us
    dot_general x95 -> x0, matrix products: 344 us -> none  [the longest x5 52.3 us: layer_backward(): jnp.einsum('tsd,fd->tsf', grad_full, w_fc2, preferred_element_type=jnp.fl...]
    all_gather x20 -> x2, waiting for transfers between devices: 391 us -> 102 us  [the longest x1 64 us: shards(): mlp_w = lax.all_gather(mlp_shard, everyone, axis=0, tiled=False)]
    reduce_scatter x10 -> x3, waiting for transfers between devices: 214 us -> 442 us  [the longest x1 182 us: shards(): lax.psum_scatter(jnp.concatenate(gm, axis=0), everyone, scatter_dimension...]
    another operation x71 -> x1, local copies, waits for them, and re-layouts: 169 us -> 1.48 us  [shards(): boundary[0].reshape(micro, quarter, 2, images, D).transpose(2, 0, 3, 1, 4)]
    pallas_call x0 -> x8, Pallas kernels: none -> 162 us  [the longest x2 47 us: attn_backward(): call(functools.partial(attn_backward_kernel, layer, images), f'attn_backw...]
    unnamed x587 -> x28, local copies, waits for them, and re-layouts: 98.4 us -> 7.68 us
    slice x100 -> x8, local copies, waits for them, and re-layouts: 71.1 us -> 5 us  [the longest x1 1.63 us: shards(): gm[None, :D // n_dp]]
  transfers between devices with their start and end apart: 63 -> 7, of which waited for: 53 -> 5; matrix products, arithmetic and copies ran while one was open for 13% -> 4% of each run, Pallas kernels for 0% -> 3%
where the time goes in v1:
time: 812 us; the launch traced here: 810 us
  waiting for transfers between devices  543 us (67%)
  Pallas kernels  162 us (20%)
  local copies, waits for them, and re-layouts  37.3 us (5%)
  blocking collectives  24.1 us (3%)
  other arithmetic  20.7 us (3%)
  between operations  14.1 us (2%)
  starting transfers between devices  9.06 us (1%)
    reduce_scatter x1, waiting for transfers between devices, shards(): lax.psum_scatter(jnp.concatenate(gm, axis=0), everyone, scatter_dimension...  182 us
    reduce_scatter x1, waiting for transfers between devices, shards(): lax.psum_scatter(jnp.concatenate(ga, axis=0), everyone, scatter_dimension...  140 us
    reduce_scatter x1, waiting for transfers between devices, shards(): lax.psum_scatter(sums.reshape((-1,) + sums.shape[2:]), everyone, scatter_...  120 us
    all_gather x1, waiting for transfers between devices, shards(): mlp_w = lax.all_gather(mlp_shard, everyone, axis=0, tiled=False)  64 us
    pallas_call x2, Pallas kernels, attn_backward(): call(functools.partial(attn_backward_kernel, layer, images), f'attn_backw...  47 us
    pallas_call x2, Pallas kernels, mlp_backward(): call(functools.partial(mlp_backward_kernel, layer, images), f'mlp_backwar...  41.7 us
    pallas_call x2, Pallas kernels, attn_forward(): call(functools.partial(attn_forward_kernel, layer, images), f'attn_forwar...  41.2 us
    all_gather x1, waiting for transfers between devices, shards(): attn_w = lax.all_gather(attn_shard, everyone, axis=0, tiled=False)  37.5 us
  transfers between devices with their start and end apart: 7, of which 5 were waited for; matrix products, arithmetic and copies ran while one was open for 4% of the time, Pallas kernels for 3%

profile of v1, /device:TPU:0, one launch (start us, length us, event | category | flops | bytes accessed | tf_op | source)
XLA Modules:
  0.0 810.2 jit_solution(342306842478501529)
XLA Ops:
  10.9 1.6 pad_maximum_fusion.3
  12.6 1.5 copy.45
  14.1 5.2 all-to-all-start
  19.5 24.1 %all-gather = bf16[128,128]{1,0:T(8,128)(2,1)S(1)} all-gather(bf16[16,128]{1,0:T(8,128)(2,1)S(1)} %maximum_maximum_fusion), channel_id=2, replica_groups=mesh['section'=2,'dp'=4,'tensor'=4] {'section','dp'}, dimensions={0}, use_global_device_ids=true | all-gather | bytes 36864 | tf_op jit(solution)/shard_map/all_gather | solution.py:513
  47.9 37.5 %all-gather.6.cloned.1.call-done = bf16[4096,512]{0,1:T(8,128)(2,1)} async-done(((bf16[128,512]{0,1:T(8,128)(2,1)}), bf16[4096,512]{0,1:T(8,128)(2,1)}) %all-gather.6.cloned.1.call-update) | async-done | bytes 4194320 | tf_op jit(solution)/shard_map/all_gather | solution.py:510
  85.4 6.5 copy.48
  91.9 20.9 %attn_forward_0.1 = (bf16[768,512]{1,0:T(8,128)(2,1)}, bf16[768,512]{1,0:T(8,128)(2,1)}, bf16[768,1536]{1,0:T(8,128)(2,1)}, bf16[12,2,64,512]{3,2,1,0:T(8,128)(2...) custom-call(bf16[4,3,49,512]{3,2,1,0:T(8,128)(2,1)} %get-tuple-element.93.source, ...), custom_call_target="tpu_custom_call" | custom-call | flops 4831838208 | bytes 12582912 | tf_op jit(solution)/shard_map/attn_forward_0/pallas_call | solution.py:399
  112.8 64.0 %all-gather.8.cloned.1.call-done = bf16[8192,512]{0,1:T(8,128)(2,1)} async-done(((bf16[256,512]{0,1:T(8,128)(2,1)}), bf16[8192,512]{0,1:T(8,128)(2,1)}) %all-gather.8.cloned.1.call-update) | async-done | bytes 8388624 | tf_op jit(solution)/shard_map/all_gather | solution.py:511
  176.8 12.0 %copy.50 = bf16[8192,512]{1,0:T(8,128)(2,1)} copy(bf16[8192,512]{0,1:T(8,128)(2,1)} %all-gather.8.cloned.1.call-done) | data formatting | bytes 16777216 | tf_op jit(solution)/shard_map/all_gather | solution.py:511
  188.9 15.5 %mlp_forward_0.1 = (bf16[768,512]{1,0:T(8,128)(2,1)}, bf16[768,2048]{1,0:T(8,128)(2,1)}, bf16[768,2048]{1,0:T(8,128)(2,1)}, bf16[768,512]{1,0:T(8,128)(2,1)}) custom-call(f32[3]{0:T(128)} %compare_convert_fusion.keep, f32[768,512]{1,0:T(8,128)} %get-tuple-element.39.mid, bf16[256,256]{1,0:T(8,128)(2,1)} %constant.36.clone.perm, f32[16,512]{1,0:T(8,128)} %bitcast.81, ...), custom_call_target="tpu_custom_call" | custom-call | flops 9663676416 | bytes 14680064 | tf_op jit(solution)/shard_map/mlp_forward_0/pallas_call | solution.py:419
  204.4 20.3 %attn_forward_1.1 = (bf16[768,512]{1,0:T(8,128)(2,1)}, bf16[768,512]{1,0:T(8,128)(2,1)}, bf16[768,1536]{1,0:T(8,128)(2,1)}, bf16[12,2,64,512]{3,2,1,0:T(8,128)(2...) custom-call(bf16[768,512]{1,0:T(8,128)(2,1)} %get-tuple-element.40.source, bf16[256,256]{1,0:T(8,128)(2,1)} %constant.36.clone.perm, ...), custom_call_target="tpu_custom_call" | custom-call | flops 4831838208 | bytes 12582912 | tf_op jit(solution)/shard_map/attn_forward_1/pallas_call | solution.py:399
  224.7 16.1 %mlp_forward_1.1 = (bf16[768,512]{1,0:T(8,128)(2,1)}, bf16[768,2048]{1,0:T(8,128)(2,1)}, bf16[768,2048]{1,0:T(8,128)(2,1)}, bf16[4,3,49,512]{3,2,1,0:T(8,128)(2,1)}) custom-call(f32[3]{0:T(128)} %compare_convert_fusion.keep, f32[768,512]{1,0:T(8,128)} %get-tuple-element.41.mid, bf16[4,49,256]{2,1,0:T(8,128)(2,1)} %constant.35.clone.perm, ...), custom_call_target="tpu_custom_call" | custom-call | flops 9663676416 | bytes 14680064 | tf_op jit(solution)/shard_map/mlp_forward_1/pallas_call | solution.py:419
  240.8 21.1 %mlp_backward_1.1 = (f32[768,512]{1,0:T(8,128)}, bf16[16,256,512]{2,1,0:T(8,128)(2,1)}, f32[16,512]{1,0:T(8,128)}) custom-call(f32[3]{0:T(128)} %compare_convert_fusion.keep, bf16[4,3,49,512]{3,2,1,0:T(8,128)(2,1)} %get-tuple-element.92.source, bf16[4,256,49]{2,1,0:T(8,128)(2,1)} %constant.34.clone.perm, f32[768,512]{1,0:T(8,128)} %get-tuple-element.41.mid, ...), custom_call_target="tpu_custom_call" | custom-call | flops 12884901888 | bytes 20971520 | tf_op jit(solution)/shard_map/mlp_backward_1/pallas_call | solution.py:434
  261.9 23.1 %attn_backward_1.1 = (bf16[768,512]{1,0:T(8,128)(2,1)}, bf16[16,128,512]{2,1,0:T(8,128)(2,1)}, f32[16,512]{1,0:T(8,128)}) custom-call(f32[768,512]{1,0:T(8,128)} %get-tuple-element.45.mid_grad, bf16[768,512]{1,0:T(8,128)(2,1)} %get-tuple-element.46.x_in, bf16[768,512]{1,0:T(8,128)(2,1)} %get-tuple-element.47.a_in, bf16[768,1536]{1,0:T(8,128)(2,1)} %get-tuple-element.48.qkv, ...), custom_call_target="tpu_custom_call" | custom-call | flops 12884901888 | bytes 16777216 | tf_op jit(solution)/shard_map/attn_backward_1/pallas_call | solution.py:451
  285.8 20.6 %mlp_backward_0.1 = (f32[768,512]{1,0:T(8,128)}, bf16[16,256,512]{2,1,0:T(8,128)(2,1)}, f32[16,512]{1,0:T(8,128)}) custom-call(f32[3]{0:T(128)} %compare_convert_fusion.keep, bf16[768,512]{1,0:T(8,128)(2,1)} %get-tuple-element.51.source, bf16[256,256]{1,0:T(8,128)(2,1)} %constant.37.clone.perm, f32[768,512]{1,0:T(8,128)} %get-tuple-element.39.mid, ...), custom_call_target="tpu_custom_call" | custom-call | flops 12884901888 | bytes 20971520 | tf_op jit(solution)/shard_map/mlp_backward_0/pallas_call | solution.py:434
  306.4 24.0 %attn_backward_0.1 = (bf16[4,3,49,512]{3,2,1,0:T(8,128)(2,1)}, bf16[16,128,512]{2,1,0:T(8,128)(2,1)}, f32[16,512]{1,0:T(8,128)}) custom-call(f32[768,512]{1,0:T(8,128)} %get-tuple-element.55.mid_grad, bf16[768,512]{1,0:T(8,128)(2,1)} %get-tuple-element.56.x_in, bf16[768,512]{1,0:T(8,128)(2,1)} %get-tuple-element.57.a_in, ...), custom_call_target="tpu_custom_call" | custom-call | flops 12884901888 | bytes 16777216 | tf_op jit(solution)/shard_map/attn_backward_0/pallas_call | solution.py:451
  332.3 3.9 pad_maximum_fusion.1
  336.3 7.5 pad_maximum_fusion
  346.3 3.7 all-to-all-start.1
  349.9 119.6 %reduce-scatter.8.cloned.1.call-done = f32[1,12,32]{2,1,0:T(8,128)} async-done(((f32[32,12,32]{2,1,0:T(8,128)}), f32[1,12,32]{2,1,0:T(8,128)}) %reduce-scatter.8.cloned.1.call-update) | async-done | bytes 1552 | tf_op jit(solution)/shard_map/reduce_scatter | solution.py:523
  472.5 3.0 copy.51
  475.4 140.5 %reduce-scatter.4.cloned.1.call-done = bf16[1,128,512]{2,1,0:T(8,128)(2,1)} async-done(((bf16[32,128,512]{2,1,0:T(8,128)(2,1)}), bf16[1,128,512]{2,1,0:T(8,128)(2,1)}) %reduce-scatter.4.cloned.1.call-update) | async-done | bytes 131088 | tf_op jit(solution)/shard_map/reduce_scatter | solution.py:518
  618.5 181.6 %reduce-scatter.6.cloned.1.call-done = bf16[1,256,512]{2,1,0:T(8,128)(2,1)} async-done(((bf16[32,256,512]{2,1,0:T(8,128)(2,1)}), bf16[1,256,512]{2,1,0:T(8,128)(2,1)}) %reduce-scatter.6.cloned.1.call-update) | async-done | bytes 262160 | tf_op jit(solution)/shard_map/reduce_scatter | solution.py:519
  802.0 1.6 slice.65
  (65 shorter events, 20.7 us)
Async XLA Ops:
  7.2 37.7 %copy-start = (s32[4,1]{0,1:T(1,128)S(1)}, s32[4,1]{0,1:T(1,128)}, u32[]{:S(2)}) copy-start(s32[4,1]{0,1:T(1,128)} %param.15) | copy-start | bytes 52
  7.2 5.4 copy-start.3
  7.2 78.2 %all-gather.6.cloned.1.call-start = ((), (), s32[]{:S(2)}) async-start(), calls=%async_computation.8 | async-start | bytes 4325376 | tf_op jit(solution)/shard_map/all_gather | solution.py:510
  9.8 167.0 %all-gather.8.cloned.1.call-start = ((), (), s32[]{:S(2)}) async-start(), calls=%async_computation.9 | async-start | bytes 8650752 | tf_op jit(solution)/shard_map/all_gather | solution.py:511
  12.5 6.8 copy-start.8
  12.6 6.8 copy-start.9
  14.1 32.6 %all-to-all-start = ((bf16[8,3,49,512]{3,2,1,0:T(8,128)(2,1)}), bf16[8,3,49,512]{3,2,1,0:T(8,128)(2,1)S(1)}, u32[]{:S(2)}, u32[]{:S(2)}) async-start(bf16[8,3,49,512]{3,2,1,0:T(8,128)(2,1)} %bitcast.3), calls=%async_computation | async-start | bytes 2752512 | tf_op jit(solution)/shard_map/all_to_all | solution.py:503
  19.3 450.3 %reduce-scatter.8.cloned.1.call-start = ((), (), s32[]{:S(2)}) async-start(), calls=%async_computation.7 | async-start | bytes 270336 | tf_op jit(solution)/shard_map/reduce_scatter | solution.py:523
  261.9 23.1 %copy-start.7 = (f32[16,512]{1,0:T(8,128)S(1)}, f32[16,512]{1,0:T(8,128)}, u32[]{:S(2)}) copy-start(f32[16,512]{1,0:T(8,128)} %get-tuple-element.70) | copy-start | bytes 98308
  306.4 24.0 %copy-start.6 = (f32[16,512]{1,0:T(8,128)S(1)}, f32[16,512]{1,0:T(8,128)}, u32[]{:S(2)}) copy-start(f32[16,512]{1,0:T(8,128)} %get-tuple-element.68) | copy-start | bytes 98308
  306.4 25.8 %copy-start.2 = (bf16[16,128,512]{2,1,0:T(8,128)(2,1)S(1)}, bf16[16,128,512]{2,1,0:T(8,128)(2,1)}, u32[]{:S(2)}) copy-start(bf16[16,128,512]{2,1,0:T(8,128)(2,1)} %get-tuple-element.64) | copy-start | bytes 6291460
  332.2 283.7 %reduce-scatter.4.cloned.1.call-start = ((), (), s32[]{:S(2)}) async-start(), calls=%async_computation.5 | async-start | bytes 4325376 | tf_op jit(solution)/shard_map/reduce_scatter | solution.py:518
  336.2 463.9 %reduce-scatter.6.cloned.1.call-start = ((), (), s32[]{:S(2)}) async-start(), calls=%async_computation.6 | async-start | bytes 8650752 | tf_op jit(solution)/shard_map/reduce_scatter | solution.py:519
  343.7 1.1 copy-start.4
  343.7 1.3 copy-start.5
  346.3 125.8 %all-to-all-start.1 = ((bf16[8,3,49,512]{3,2,1,0:T(8,128)(2,1)}), bf16[8,3,49,512]{3,2,1,0:T(8,128)(2,1)S(1)}, u32[]{:S(2)}, u32[]{:S(2)}) async-start(bf16[8,3,49,512]{3,2,1,0:T(8,128)(2,1)} %pad_maximum_fusion.2), calls=%async_computation.1 | async-start | bytes 2752512 | tf_op jit(solution)/shard_map/all_to_all | solution.py:525
  472.5 331.2 %copy-start.1 = (s32[4,1]{0,1:T(1,128)S(1)}, s32[4,1]{0,1:T(1,128)}, u32[]{:S(2)}) copy-start(s32[4,1]{0,1:T(1,128)} %param.15) | copy-start | bytes 52
Sparse Core Ops, SparseCore 0:
  11.4 73.9 all-gather.5
  88.8 87.9 all-gather.7
  332.4 137.1 reduce-scatter.7
  471.7 144.1 reduce-scatter.3
  618.0 182.0 reduce-scatter.5
